TPU v7x, 32 devices: a whole 2x2x4 slice. The times are simulated.
32 devices in a mesh: clip: 8 (over y, x, core), tm: 4 (over z).
Axes of the slice: x: 2, y: 2, z: 4, core: 2. Of those that a mesh axis runs over, the one named last changes fastest.
Arguments:
- latent: bfloat16 [8, 32, 8, 32, 16], P('clip', 'tm'), may hold values from -6 to 6
- offsets: int32 [8], P('clip'), may hold values from 0 to 16
- teacher: bfloat16 [8, 32, 8, 16, 384], P('clip', 'tm'), may hold values from -6 to 6
- w_in: bfloat16 [432, 384], replicated, may hold values from -0.3125 to 0.3125
- w_mid: bfloat16 [10368, 384], P('clip'), may hold values from -0.0625 to 0.0625
Outputs:
- grad_mid: float32 [10368, 384], P('clip')
- grad_in: float32 [432, 384], replicated
Inputs may be any that keep to these rules, and one draw needn't show every extreme that they name: `offsets`: each clip's crop start among the latent columns.
All inputs are finite; a program needn't handle non-finite values.
Results may differ from a plain program's by a relative error of at most 0.00095.
Values may be sent and summed in bfloat16 or wider, within the bound.
No kernel may reach another device: no remote copies, remote signals or barrier semaphores. Data moves between devices by JAX's collectives and lax.ppermute only.
A program may use at most 192 MiB of HBM per device.

v0:
```python
import math
import jax
import jax.numpy as jnp
from jax import lax
from jax.sharding import PartitionSpec as P


def passed_along(block, axis, distance):
    devices = range(lax.axis_size(axis))
    route = [(i - distance, i) for i in devices if i - distance in devices]
    return lax.ppermute(block, axis, route)


def tap_masks(count, rows, cols):
    place = jnp.arange(count, dtype=jnp.int32) % (rows * cols)
    row_pos = place // cols
    col_pos = place % cols
    masks = []
    for row_off in range(3):
        for col_off in range(3):
            good_row = (row_pos + row_off - 1 >= 0) & (row_pos + row_off - 1 < rows)
            good_col = (col_pos + col_off - 1 >= 0) & (col_pos + col_off - 1 < cols)
            masks.append((good_row & good_col).astype(jnp.bfloat16).reshape(count, 1))
    return masks


def tap_slices(extended, count, rows, cols, masks):
    margin = jnp.zeros((cols + 1, extended.shape[1]), extended.dtype)
    padded = jnp.concatenate([margin, extended, margin], axis=0)
    plane = rows * cols
    pieces = []
    for depth in range(3):
        for row_off in range(3):
            for col_off in range(3):
                first = depth * plane + row_off * cols + col_off
                pieces.append(padded[first : first + count] * masks[row_off * 3 + col_off])
    return pieces


def cross_dot(left, right):
    return lax.dot_general(
        left, right, (((0,), (0,)), ((), ())), preferred_element_type=jnp.float32
    )


def shards(latent, offsets, teacher, w_in, w_mid):
    frames = teacher.shape[1]
    rows = teacher.shape[2]
    cols = teacher.shape[3]
    chans = teacher.shape[4]
    plane = rows * cols
    count = frames * plane
    lat_chans = latent.shape[4]
    total_cells = lax.axis_size("clip") * lax.axis_size("tm") * count
    scale = 2.0 / math.sqrt(total_cells)
    masks = tap_masks(count, rows, cols)
    crop = lax.dynamic_slice_in_dim(latent[0], offsets[0], cols, axis=2).reshape(count, lat_chans)
    earlier = passed_along(crop[count - 2 * plane :], "tm", 1)
    crop_ext = jnp.concatenate([earlier, crop], axis=0)
    patch_in = jnp.concatenate(tap_slices(crop_ext, count, rows, cols, masks), axis=1)
    z_first = jnp.dot(patch_in, w_in, preferred_element_type=jnp.float32)
    act = jax.nn.silu(z_first).astype(jnp.bfloat16)
    act_prev = passed_along(act[count - 2 * plane :], "tm", 1)
    act_ext = jnp.concatenate([act_prev, act], axis=0)
    act_taps = tap_slices(act_ext, count, rows, cols, masks)
    w_full = lax.all_gather(w_mid, "clip", axis=0, tiled=True)
    output = jnp.zeros((count, chans), jnp.float32)
    for k in range(27):
        output = output + jnp.dot(
            act_taps[k], w_full[k * chans : (k + 1) * chans], preferred_element_type=jnp.float32
        )
    target_rows = teacher[0].reshape(count, chans).astype(jnp.float32)
    grad_low = ((output - target_rows) * scale).astype(jnp.bfloat16)
    local_mid = jnp.concatenate([cross_dot(act_taps[k], grad_low) for k in range(27)], axis=0)
    lead = 2 * plane + cols + 1
    masked_pads = []
    for k in range(9):
        masked_pads.append(jnp.pad(grad_low * masks[k], ((lead, lead), (0, 0))))
    ext_count = count + 2 * plane
    adjoint = jnp.zeros((ext_count, chans), jnp.float32)
    for depth in range(3):
        for row_off in range(3):
            for col_off in range(3):
                k = depth * 9 + row_off * 3 + col_off
                first = (2 - depth) * plane + (2 - row_off) * cols + (2 - col_off)
                piece = masked_pads[row_off * 3 + col_off][first : first + ext_count]
                adjoint = adjoint + lax.dot_general(
                    piece,
                    w_full[k * chans : (k + 1) * chans],
                    (((1,), (1,)), ((), ())),
                    preferred_element_type=jnp.float32,
                )
    outgoing = adjoint[: 2 * plane]
    incoming = passed_along(outgoing.astype(jnp.bfloat16), "tm", -1).astype(outgoing.dtype)
    own = adjoint[2 * plane :]
    dact = jnp.concatenate([own[: count - 2 * plane], own[count - 2 * plane :] + incoming], axis=0)
    sig = jax.nn.sigmoid(z_first)
    dz_first = (dact * sig * (1.0 + z_first * (1.0 - sig))).astype(jnp.bfloat16)
    grad_in = lax.psum(cross_dot(patch_in, dz_first), ("clip", "tm"))
    summed = lax.psum(local_mid, "tm")
    grad_mid = lax.psum_scatter(summed, "clip", scatter_dimension=0, tiled=True)
    return (grad_mid, grad_in)


def solution(mesh):
    return jax.shard_map(
        shards,
        mesh=mesh,
        in_specs=(
            P("clip", "tm", None, None, None),
            P("clip"),
            P("clip", "tm", None, None, None),
            P(),
            P("clip", None),
        ),
        out_specs=(P("clip", None), P()),
        check_vma=False,
    )
```

profile of v0, /device:TPU:0, one launch (start us, length us, event | category | flops | bytes accessed | tf_op | source)
XLA Modules:
  0.0 524.9 jit_solution(12850490637867089896)
XLA Ops:
  9.7 4.9 collective-permute-start
  18.5 2.0 multiply_convert_fusion
  20.5 3.9 collective-permute-start.1
  24.4 3.4 collective-permute-done.1
  27.8 2.3 concatenate.47
  30.2 35.1 %all-gather.2.cloned.1.call-done = bf16[10368,384]{1,0:T(8,128)(2,1)} async-done(((bf16[1296,384]{1,0:T(8,128)(2,1)}), bf16[10368,384]{1,0:T(8,128)(2,1)}) %all-gather.2.cloned.1.call-update) | async-done | bytes 7962640 | tf_op jit(solution)/shard_map/all_gather | solution.py:66
  65.3 3.0 fusion.52
  68.3 2.8 fusion.51
  71.1 2.8 fusion.50
  73.9 1.9 fusion.49
  75.8 1.9 fusion.132
  77.7 1.9 fusion.129
  79.5 1.9 fusion.126
  81.4 1.9 fusion.123
  83.3 1.8 fusion.120
  85.2 1.8 fusion.117
  87.0 1.9 fusion.114
  88.9 1.9 fusion.111
  90.7 1.9 fusion.108
  92.7 1.8 fusion.105
  94.5 1.9 fusion.102
  96.4 2.0 fusion.99
  98.4 1.9 fusion.96
  100.2 2.1 fusion.93
  102.3 1.9 fusion.90
  104.2 1.9 fusion.87
  106.1 1.9 fusion.84
  108.0 1.9 fusion.46
  109.9 1.9 fusion.47
  111.8 1.9 fusion.48
  113.7 1.9 fusion.45
  115.6 1.8 fusion.43
  117.4 17.8 %broadcast_multiply_fusion = (bf16[1024,384]{1,0:T(8,128)(2,1)S(1)}, bf16[1024,384]{1,0:T(8,128)(2,1)S(1)}, bf16[1024,384]{1,0:T(8,128)(2,1)S(1)}, bf16[1024,384...) fusion(bf16[1024]{0:T(1024)(128)(2,1)S(1)} %get-tuple-element.1, ...), kind=kOutput, calls=%fused_computation.165 | convolution fusion | flops 319684608 | bytes 50843648 | tf_op jit(solution)/shard_map/dot_general | solution.py:69
  135.3 3.1 convolution_dynamic-update-slice_fusion.26
  156.4 1.7 convolution_dynamic-update-slice_fusion.14
  159.7 1.7 convolution_dynamic-update-slice_fusion.12
  164.6 1.7 convolution_dynamic-update-slice_fusion.9
  171.2 1.9 convolution_dynamic-update-slice_fusion.5
  181.4 2.0 fusion.4
  183.5 1.9 convolution_add_fusion.25
  185.4 1.9 convolution_add_fusion.24
  187.3 1.9 convolution_add_fusion.23
  210.1 7.5 %collective-permute-done.2 = bf16[256,384]{1,0:T(8,128)(2,1)S(1)} collective-permute-done((bf16[256,384]{1,0:T(8,128)(2,1)S(1)}, bf16[256,384]{1,0:T(8,128)(2,1)S(1)}, u32[]{:S(2)}, u32[]{:S(2)}) %collective-permute-start.2) | collective-permute-done | bytes 196640 | tf_op jit(solution)/shard_map/ppermute | solution.py:11
  217.7 1.8 fusion.40
  219.6 74.8 %reduce-scatter.2.cloned.1.call-done = f32[1296,384]{1,0:T(8,128)} async-done(((f32[10368,384]{1,0:T(8,128)}), f32[1296,384]{1,0:T(8,128)}) %reduce-scatter.2.cloned.1.call-update) | async-done | bytes 1990672 | tf_op jit(solution)/shard_map/reduce_scatter | solution.py:101
  294.4 133.7 %all-reduce.14.cloned.1.call-done = f32[432,384]{1,0:T(8,128)} async-done(((f32[432,384]{1,0:T(8,128)}), f32[432,384]{1,0:T(8,128)}) %all-reduce.14.cloned.1.call-update) | async-done | bytes 663568 | tf_op jit(solution)/shard_map/psum | solution.py:99
  428.1 86.2 %all-reduce.16.cloned.1.call-done = f32[1296,384]{1,0:T(8,128)} async-done(((f32[1296,384]{1,0:T(8,128)}), f32[1296,384]{1,0:T(8,128)}) %all-reduce.16.cloned.1.call-update) | async-done | bytes 1990672 | tf_op jit(solution)/shard_map/psum | solution.py:100
  514.3 3.0 copy.65
  (141 shorter events, 63.2 us)
Async XLA Ops:
  7.2 11.3 %copy-start = (bf16[432,384]{1,0:T(8,128)(2,1)S(1)}, bf16[432,384]{1,0:T(8,128)(2,1)}, u32[]{:S(2)}) copy-start(bf16[432,384]{1,0:T(8,128)(2,1)} %param.8) | copy-start | bytes 995332
  7.2 58.1 %all-gather.2.cloned.1.call-start = ((), (), s32[]{:S(2)}) async-start(), calls=%async_computation.1 | async-start | bytes 8957952 | tf_op jit(solution)/shard_map/all_gather | solution.py:66
  7.9 286.4 %reduce-scatter.2.cloned.1.call-start = ((), (), s32[]{:S(2)}) async-start(), calls=%async_computation.3 | async-start | bytes 17915904 | tf_op jit(solution)/shard_map/reduce_scatter | solution.py:101
  9.7 6.6 %collective-permute-start = (bf16[256,16]{0,1:T(8,128)(2,1)S(1)}, bf16[256,16]{0,1:T(8,128)(2,1)S(1)}, u32[]{:S(2)}, u32[]{:S(2)}) collective-permute-start(bf16[256,16]{0,1:T(8,128)(2,1)S(1)} %slice.384), channel_id=1, source_target_pairs={{0,1},{1,2},{2,3},{4,5},{5,6},{6,7},{8,9},{9,10},{10,11},{12,13},{... | collective-permute-start | bytes 24584 | tf_op jit(solution)/shard_map/ppermute | solution.py:11
  18.5 2.0 copy-start.13
  20.5 7.4 %collective-permute-start.1 = (bf16[256,384]{1,0:T(8,128)(2,1)S(1)}, bf16[256,384]{1,0:T(8,128)(2,1)S(1)}, u32[]{:S(2)}, u32[]{:S(2)}) collective-permute-start(bf16[256,384]{1,0:T(8,128)(2,1)S(1)} %slice.517), channel_id=1, source_target_pairs={{0,1},{1,2},{2,3},{4,5},{5,6},{6,7},{8,9},{9,10},{10,11},{12,13},{... | collective-permute-start | bytes 589832 | tf_op jit(solution)/shard_map/ppermute | solution.py:11
  30.2 43.8 %copy-start.9 = (bf16[1297,384]{1,0:T(8,128)(2,1)}, bf16[1297,384]{1,0:T(8,128)(2,1)S(1)}, u32[]{:S(2)}) copy-start(bf16[1297,384]{1,0:T(8,128)(2,1)S(1)} %concatenate.47) | copy-start | bytes 2988292
  65.3 8.7 %copy-start.2 = (bf16[10368,384]{1,0:T(8,128)(2,1)S(1)}, bf16[10368,384]{1,0:T(8,128)(2,1)}, u32[]{:S(2)}) copy-start(bf16[10368,384]{1,0:T(8,128)(2,1)} %all-gather.2.cloned.1.call-done) | copy-start | bytes 23887876
  135.3 3.1 copy-start.10
  135.3 3.1 copy-start.11
  181.3 2.1 copy-start.7
  181.3 246.8 %all-reduce.14.cloned.1.call-start = ((), (), s32[]{:S(2)}) async-start(), calls=%async_computation.2 | async-start | bytes 1327104 | tf_op jit(solution)/shard_map/psum | solution.py:99
  183.4 1.9 copy-start.6
  183.4 5.7 %slice-start = ((s8[7962624]{0:T(1024)(128)(4,1)}), s8[4194304]{0:T(1024)(128)(4,1)S(1)}, s32[]{:S(2)}) async-start(s8[7962624]{0:T(1024)(128)(4,1)} %bitcast.44), calls=%async_computation.5 | async-start | bytes 8388608
  185.4 1.9 copy-start.5
  185.4 3.8 slice-start.1
  187.3 1.9 copy-start.4
  189.2 1.3 copy-start.3
  192.8 1.3 copy-start.8
  208.5 9.2 %copy-start.14 = (bf16[1024,432]{0,1:T(8,128)(2,1)S(1)}, bf16[1024,432]{0,1:T(8,128)(2,1)}, u32[]{:S(2)}) copy-start(bf16[1024,432]{0,1:T(8,128)(2,1)} %copy-done.13) | copy-start | bytes 2654212
  208.5 9.2 %copy-start.15 = (f32[1024,384]{1,0:T(8,128)S(1)}, f32[1024,384]{1,0:T(8,128)}, u32[]{:S(2)}) copy-start(f32[1024,384]{1,0:T(8,128)} %get-tuple-element.12) | copy-start | bytes 4718596
  208.5 9.2 %collective-permute-start.2 = (bf16[256,384]{1,0:T(8,128)(2,1)S(1)}, bf16[256,384]{1,0:T(8,128)(2,1)S(1)}, u32[]{:S(2)}, u32[]{:S(2)}) collective-permute-start(bf16[256,384]{1,0:T(8,128)(2,1)S(1)} %slice.1014), channel_id=1, source_target_pairs={{1,0},{2,1},{3,2},{5,4},{6,5},{7,6},{9,8},{10,9},{11,10},{13,12},{... | collective-permute-start | bytes 589832 | tf_op jit(solution)/shard_map/ppermute | solution.py:11
  219.5 294.8 %all-reduce.16.cloned.1.call-start = ((), (), s32[]{:S(2)}) async-start(), calls=%async_computation.4 | async-start | bytes 3981312 | tf_op jit(solution)/shard_map/psum | solution.py:100
  428.1 89.2 %copy-start.12 = (f32[432,384]{1,0:T(8,128)S(1)}, f32[432,384]{1,0:T(8,128)}, u32[]{:S(2)}) copy-start(f32[432,384]{1,0:T(8,128)} %all-reduce.14.cloned.1.call-done) | copy-start | bytes 1990660
  514.3 3.9 copy-start.1
Sparse Core Ops, SparseCore 0:
  9.9 55.3 all-gather.1
  181.4 112.8 reduce-scatter.1
  301.0 127.0 all-reduce.13
  430.4 83.9 all-reduce.15
where the time goes:
time: 528 us; the launch traced here: 525 us
  waiting for transfers between devices  342 us (65%)
  matrix products  145 us (27%)
  between operations  15.4 us (3%)
  starting transfers between devices  10.6 us (2%)
  local copies, waits for them, and re-layouts  10 us (2%)
    psum x1, waiting for transfers between devices, shards(): grad_in = lax.psum(cross_dot(patch_in, dz_first), ('clip', 'tm'))  134 us
    psum x1, waiting for transfers between devices, shards(): summed = lax.psum(local_mid, 'tm')  86.2 us
    reduce_scatter x1, waiting for transfers between devices, shards(): grad_mid = lax.psum_scatter(summed, 'clip', scatter_dimension=0, tiled=True)  74.8 us
    dot_general x27, matrix products, shards(): jnp.dot(act_taps[k], w_full[k * chans:(k + 1) * chans], preferred_element...  70 us
    dot_general x28, matrix products, cross_dot(): lax.dot_general(left, right, (((0,), (0,)), ((), ())), preferred_element_...  47.7 us
    all_gather x1, waiting for transfers between devices, shards(): w_full = lax.all_gather(w_mid, 'clip', axis=0, tiled=True)  35.1 us
    dot_general x27, matrix products, shards(): lax.dot_general(piece, w_full[k * chans:(k + 1) * chans], (((1,), (1,)),...  25.7 us
    ppermute x3, waiting for transfers between devices, passed_along(): return lax.ppermute(block, axis, route)  11 us
  transfers between devices with their start and end apart: 7, of which 6 were waited for; matrix products, arithmetic and copies ran while one was open for 7% of the time, Pallas kernels for 0%

commit v1 on v0

--- a/solution.py
+++ b/solution.py
@@ -97,7 +97,9 @@
     sig = jax.nn.sigmoid(z_first)
     dz_first = (dact * sig * (1.0 + z_first * (1.0 - sig))).astype(jnp.bfloat16)
     grad_in = lax.psum(cross_dot(patch_in, dz_first), ("clip", "tm"))
-    summed = lax.psum(local_mid, "tm")
+    summed = local_mid
+    for hop in (1, 2):
+        summed = summed + lax.ppermute(summed, "tm", [(dev, dev ^ hop) for dev in range(4)])
     grad_mid = lax.psum_scatter(summed, "clip", scatter_dimension=0, tiled=True)
     return (grad_mid, grad_in)
 

time: 528 us -> 1470 us (2.78)
  waiting for transfers between devices: 342 us -> 1270 us
  other arithmetic: 2.07 us -> 30.5 us
  matrix products: 145 us -> 118 us
    ppermute x0 -> x2, waiting for transfers between devices: none -> 994 us  [shards(): lax.ppermute(summed, 'tm', [(dev, dev ^ hop) for dev in range(4)])]
    psum x1 -> x0, waiting for transfers between devices: 86.2 us -> none  [shards(): summed = lax.psum(local_mid, 'tm')]
    reduce_scatter x1, waiting for transfers between devices: 74.8 us -> 119 us  [shards(): grad_mid = lax.psum_scatter(summed, 'clip', scatter_dimension=0, tiled=True)]
    add x0 -> x2, other arithmetic: none -> 28.4 us  [shards(): summed + lax.ppermute(summed, 'tm', [(dev, dev ^ hop) for dev in range(4)])]
    dot_general x28, matrix products: 47.7 us -> 25 us  [cross_dot(): lax.dot_general(left, right, (((0,), (0,)), ((), ())), preferred_element_...]
    psum x1, waiting for transfers between devices: 134 us -> 112 us  [shards(): grad_in = lax.psum(cross_dot(patch_in, dz_first), ('clip', 'tm'))]
  transfers between devices with their start and end apart: 7 -> 8, of which waited for: 6 -> 7; matrix products, arithmetic and copies ran while one was open for 7% -> 3% of each run, Pallas kernels for 0% -> 0%
where the time goes in v1:
time: 1470 us; the launch traced here: 1460 us
  waiting for transfers between devices  1270 us (86%)
  matrix products  118 us (8%)
  other arithmetic  30.5 us (2%)
  between operations  15.5 us (1%)
    ppermute x2, waiting for transfers between devices, shards(): lax.ppermute(summed, 'tm', [(dev, dev ^ hop) for dev in range(4)])  994 us
    reduce_scatter x1, waiting for transfers between devices, shards(): grad_mid = lax.psum_scatter(summed, 'clip', scatter_dimension=0, tiled=True)  119 us
    psum x1, waiting for transfers between devices, shards(): grad_in = lax.psum(cross_dot(patch_in, dz_first), ('clip', 'tm'))  112 us
    dot_general x27, matrix products, shards(): jnp.dot(act_taps[k], w_full[k * chans:(k + 1) * chans], preferred_element...  69.9 us
    all_gather x1, waiting for transfers between devices, shards(): w_full = lax.all_gather(w_mid, 'clip', axis=0, tiled=True)  35.1 us
  transfers between devices with their start and end apart: 8, of which 7 were waited for; matrix products, arithmetic and copies ran while one was open for 3% of the time, Pallas kernels for 0%

profile of v1, /device:TPU:0, one launch (start us, length us, event | category | flops | bytes accessed | tf_op | source)
XLA Modules:
  0.0 1463.5 jit_solution(13236428776917786143)
XLA Ops:
  9.7 4.9 collective-permute-start
  14.7 1.1 constant_dynamic-slice_fusion.1
  18.5 2.0 multiply_convert_fusion
  20.5 3.9 collective-permute-start.1
  24.4 3.4 collective-permute-done.1
  27.8 2.3 concatenate.47
  30.2 35.1 %all-gather.2.cloned.1.call-done = bf16[10368,384]{1,0:T(8,128)(2,1)} async-done(((bf16[1296,384]{1,0:T(8,128)(2,1)}), bf16[10368,384]{1,0:T(8,128)(2,1)}) %all-gather.2.cloned.1.call-update) | async-done | bytes 7962640 | tf_op jit(solution)/shard_map/all_gather | solution.py:66
  65.3 3.0 fusion.52
  68.2 2.8 fusion.51
  71.1 2.8 fusion.50
  73.9 1.9 fusion.49
  75.8 1.9 fusion.132
  77.6 1.9 fusion.129
  79.5 1.9 fusion.126
  81.4 1.8 fusion.123
  83.3 1.9 fusion.120
  85.2 1.9 fusion.117
  87.1 1.9 fusion.114
  89.0 1.9 fusion.111
  90.8 1.9 fusion.108
  92.7 1.9 fusion.105
  94.6 1.9 fusion.102
  96.5 1.9 fusion.99
  98.4 1.9 fusion.96
  100.3 2.1 fusion.93
  102.4 1.8 fusion.90
  104.3 1.9 fusion.87
  106.2 1.9 fusion.84
  108.0 1.9 fusion.46
  109.9 1.9 fusion.47
  111.8 1.9 fusion.48
  113.7 1.9 fusion.45
  115.5 1.9 fusion.43
  117.4 17.9 %broadcast_multiply_fusion = (bf16[1024,384]{1,0:T(8,128)(2,1)S(1)}, bf16[1024,384]{1,0:T(8,128)(2,1)S(1)}, bf16[1024,384]{1,0:T(8,128)(2,1)S(1)}, bf16[1024,384...) fusion(bf16[1024]{0:T(1024)(128)(2,1)S(1)} %get-tuple-element.1, ...), kind=kOutput, calls=%fused_computation.165 | convolution fusion | flops 319684608 | bytes 50843648 | tf_op jit(solution)/shard_map/dot_general | solution.py:69
  135.3 2.3 convolution_dynamic-update-slice_fusion.26
  158.8 5.8 copy-done.2
  164.6 1.5 collective-permute-start.2
  166.0 342.6 %collective-permute-done.2 = f32[10368,384]{1,0:T(8,128)S(1)} collective-permute-done((f32[10368,384]{1,0:T(8,128)S(1)}, f32[10368,384]{1,0:T(8,128)S(1)}, u32[]{:S(2)}, u32[]{:S(2)}) %collective-permute-start.2) | collective-permute-done | bytes 15925280 | tf_op jit(solution)/shard_map/ppermute | solution.py:102
  508.7 11.3 add.685
  520.0 2.4 collective-permute-start.3
  545.3 1.4 collective-permute-start.4
  546.8 6.5 collective-permute-done.4
  553.4 1.8 fusion.40
  555.2 651.7 %collective-permute-done.3 = f32[10368,384]{1,0:T(8,128)} collective-permute-done((f32[10368,384]{1,0:T(8,128)}, f32[10368,384]{1,0:T(8,128)}, u32[]{:S(2)}, u32[]{:S(2)}) %collective-permute-start.3) | collective-permute-done | bytes 15925280 | tf_op jit(solution)/shard_map/ppermute | solution.py:102
  1206.9 17.2 %add.686 = f32[10368,384]{1,0:T(8,128)} add(f32[10368,384]{1,0:T(8,128)} %add.685, f32[10368,384]{1,0:T(8,128)} %collective-permute-done.3) | non-fusion elementwise | flops 3981312 | bytes 47775744 | tf_op jit(solution)/shard_map/add | solution.py:102
  1224.1 112.2 %all-reduce.13.cloned.1.call-done = f32[432,384]{1,0:T(8,128)} async-done(((f32[432,384]{1,0:T(8,128)}), f32[432,384]{1,0:T(8,128)}) %all-reduce.13.cloned.1.call-update) | async-done | bytes 663568 | tf_op jit(solution)/shard_map/psum | solution.py:99
  1336.2 118.6 %reduce-scatter.2.cloned.1.call-done = f32[1296,384]{1,0:T(8,128)} async-done(((f32[10368,384]{1,0:T(8,128)}), f32[1296,384]{1,0:T(8,128)}) %reduce-scatter.2.cloned.1.call-update) | async-done | bytes 1990672 | tf_op jit(solution)/shard_map/reduce_scatter | solution.py:103
  1454.8 2.0 copy.64
  (143 shorter events, 48.3 us)
Async XLA Ops:
  7.2 11.3 copy-start
  7.2 58.1 %all-gather.2.cloned.1.call-start = ((), (), s32[]{:S(2)}) async-start(), calls=%async_computation.1 | async-start | bytes 8957952 | tf_op jit(solution)/shard_map/all_gather | solution.py:66
  7.9 1328.3 %all-reduce.13.cloned.1.call-start = ((), (), s32[]{:S(2)}) async-start(), calls=%async_computation.3 | async-start | bytes 1327104 | tf_op jit(solution)/shard_map/psum | solution.py:99
  9.7 6.6 collective-permute-start
  18.5 2.0 copy-start.13
  20.5 7.3 collective-permute-start.1
  30.2 45.6 %copy-start.10 = (bf16[1297,384]{1,0:T(8,128)(2,1)}, bf16[1297,384]{1,0:T(8,128)(2,1)S(1)}, u32[]{:S(2)}) copy-start(bf16[1297,384]{1,0:T(8,128)(2,1)S(1)} %concatenate.47) | copy-start | bytes 2988292
  65.3 8.6 copy-start.3
  135.3 2.3 copy-start.11
  135.3 2.3 copy-start.12
  158.0 364.4 %slice-start = ((s8[7962624]{0:T(1024)(128)(4,1)}), s8[4194304]{0:T(1024)(128)(4,1)S(1)}, s32[]{:S(2)}) async-start(s8[7962624]{0:T(1024)(128)(4,1)} %bitcast.44), calls=%async_computation.4 | async-start | bytes 8388608
  158.8 5.8 copy-start.2
  164.6 357.8 %slice-start.1 = ((s8[7962624]{0:T(1024)(128)(4,1)}), s8[3768320]{0:T(1024)(128)(4,1)S(1)}, s32[]{:S(2)}) async-start(s8[7962624]{0:T(1024)(128)(4,1)} %bitcast.44), calls=%async_computation.5 | async-start | bytes 7536640
  164.6 357.8 %copy-start.9 = (bf16[1024,384]{1,0:T(8,128)(2,1)S(1)}, bf16[1024,384]{1,0:T(8,128)(2,1)}, u32[]{:S(2)}) copy-start(bf16[1024,384]{1,0:T(8,128)(2,1)} %get-tuple-element.10) | copy-start | bytes 2359300
  164.6 344.1 %collective-permute-start.2 = (f32[10368,384]{1,0:T(8,128)S(1)}, f32[10368,384]{1,0:T(8,128)S(1)}, u32[]{:S(2)}, u32[]{:S(2)}) collective-permute-start(f32[10368,384]{1,0:T(8,128)S(1)} %convolution_dynamic-update-slice_fusion), channel_id=1, source_target_pairs={{0,1},{1,0},{2,3},{3,2},{4,5},{5,4},{6,7},{7,6},{8,9},{9,8},{10,11... | collective-permute-start | bytes 47775752 | tf_op jit(solution)/shard_map/ppermute | solution.py:102
  520.0 3.2 copy-start.8
  520.0 686.9 %collective-permute-start.3 = (f32[10368,384]{1,0:T(8,128)}, f32[10368,384]{1,0:T(8,128)}, u32[]{:S(2)}, u32[]{:S(2)}) collective-permute-start(f32[10368,384]{1,0:T(8,128)} %add.685), channel_id=1, source_target_pairs={{0,2},{1,3},{2,0},{3,1},{4,6},{5,7},{6,4},{7,5},{8,10},{9,11},{10,... | collective-permute-start | bytes 47775752 | tf_op jit(solution)/shard_map/ppermute | solution.py:102
  523.2 1.1 copy-start.7
  524.3 1.1 copy-start.6
  525.4 1.1 copy-start.5
  526.6 1.1 copy-start.4
  545.3 8.1 copy-start.14
  545.3 8.1 copy-start.15
  545.3 8.0 collective-permute-start.4
  555.1 899.7 %reduce-scatter.2.cloned.1.call-start = ((), (), s32[]{:S(2)}) async-start(), calls=%async_computation.2 | async-start | bytes 17915904 | tf_op jit(solution)/shard_map/reduce_scatter | solution.py:103
  1224.1 232.7 %copy-start.1 = (bf16[432,384]{1,0:T(8,128)(2,1)S(1)}, bf16[432,384]{1,0:T(8,128)(2,1)}, u32[]{:S(2)}) copy-start(bf16[432,384]{1,0:T(8,128)(2,1)} %param.8) | copy-start | bytes 995332
Sparse Core Ops, SparseCore 0:
  9.9 55.3 all-gather.1
  555.3 780.9 all-reduce.12
  1340.9 113.8 reduce-scatter.1
